TPU v7x, 256 devices: a whole 4x4x8 slice. The times are simulated.
256 devices in a mesh: ctx: 32 (over y, z), tp: 8 (over x, core).
Axes of the slice: x: 4, y: 4, z: 8, core: 2. Of those that a mesh axis runs over, the one named last changes fastest.
Arguments:
- q_in: bfloat16 [8192, 8192], P('ctx', 'tp'), may hold values from -10.5 to 10.5
- k_in: bfloat16 [8192, 8192], P('ctx', 'tp'), may hold values from -6 to 6
- v_in: bfloat16 [8192, 8192], P('ctx', 'tp'), may hold values from -6 to 6
- grad_out: bfloat16 [8192, 8192], P('ctx', 'tp'), may hold values from -6 to 6
- doc_ids: int32 [8192], P('ctx'), may hold values from 0 to 3, never falling along the last dimension, each value on 1 to 4096 neighbouring positions
- gain: bfloat16 [8192], P('tp'), may hold values from 0.099609375 to 1.8984375
- filters: bfloat16 [512, 128], P('tp'), may hold values from -0.5 to 0.5
- short_weight: bfloat16 [3, 3, 8192], P(None, None, 'tp'), may hold values from -3.5 to 3.5
Outputs:
- grad_q: bfloat16 [8192, 8192], P('ctx', 'tp')
- grad_k: bfloat16 [8192, 8192], P('ctx', 'tp')
- grad_v: bfloat16 [8192, 8192], P('ctx', 'tp')
- grad_gain: float32 [8192], P('tp')
- grad_filters: float32 [512, 128], P('tp')
- grad_short: float32 [3, 3, 8192], P(None, None, 'tp')
Inputs may be any that keep to these rules, and one draw needn't show every extreme that they name: doc_ids never fall along the window, so every document is one run of consecutive tokens; one document covers exactly 4096 tokens.
All inputs are finite; a program needn't handle non-finite values.
Results may differ from a plain program's by a relative error of at most 0.0049.
Values may be sent and summed in bfloat16 or wider, within the bound.
A program may use at most 128 MiB of HBM per device.

v0:
```python
import math
import jax
import jax.numpy as jnp
from jax import lax
from jax.sharding import PartitionSpec as P

D = 8192
EPS = 1e-06


def shifted(value, axis, by):
    count = lax.axis_size(axis)
    pairs = [(i, i + by) for i in range(count) if 0 <= i + by < count]
    return lax.ppermute(value, axis, pairs)


def featurize(extended, weights, marks_ext, rim_edge):
    length = extended.shape[0] - rim_edge
    own_marks = marks_ext[rim_edge:]
    running = jnp.zeros((length, extended.shape[1]), jnp.float32)
    for offset in range(rim_edge + 1):
        start_row = rim_edge - offset
        agree = (marks_ext[start_row : start_row + length] == own_marks).astype(jnp.float32)[
            :, None
        ]
        running = (
            running
            + weights[offset].astype(jnp.float32)[None, :]
            * extended[start_row : start_row + length].astype(jnp.float32)
            * agree
        )
    return running


def banded(coeffs, block_rows):
    groups, taps = coeffs.shape
    span_cols = block_rows + taps - 1
    padded = jnp.concatenate([coeffs, jnp.zeros((groups, block_rows), coeffs.dtype)], axis=1)
    repeated = jnp.tile(padded, (1, block_rows))[:, : block_rows * span_cols]
    return repeated.reshape(groups, block_rows, span_cols)


def diagonal_sums(pair_grad, taps):
    groups, block_rows, span_cols = pair_grad.shape
    flat_terms = pair_grad.reshape(groups, block_rows * span_cols)
    flat_terms = jnp.concatenate([flat_terms, jnp.zeros((groups, block_rows), jnp.float32)], axis=1)
    return jnp.sum(flat_terms.reshape(groups, block_rows, span_cols + 1)[:, :, :taps], axis=1)


def unfeature(grad_feat, tail, weights, marks_after, own_marks):
    row_count = grad_feat.shape[0]
    extended = jnp.concatenate([grad_feat, tail], axis=0)
    running = jnp.zeros(grad_feat.shape, jnp.float32)
    for offset in range(weights.shape[0]):
        agree = (marks_after[offset : offset + row_count] == own_marks).astype(jnp.float32)[:, None]
        running = (
            running
            + weights[offset].astype(jnp.float32)[None, :]
            * extended[offset : offset + row_count]
            * agree
        )
    return running.astype(jnp.bfloat16)


def short_terms(grad_feat, short_in, short_marks, own_marks, rim_edge):
    row_count = grad_feat.shape[0]
    pieces = []
    for offset in range(rim_edge + 1):
        start_row = rim_edge - offset
        agree = (short_marks[start_row : start_row + row_count] == own_marks).astype(jnp.float32)[
            :, None
        ]
        pieces.append(
            jnp.sum(
                grad_feat * short_in[start_row : start_row + row_count].astype(jnp.float32) * agree,
                axis=0,
            )
        )
    return jnp.stack(pieces)


def on_device(q_in, k_in, v_in, grad_out, doc_ids, gain, filters, short_weight):
    row_count, channels = q_in.shape
    groups, taps = filters.shape
    group_width = channels // groups
    rim_edge = short_weight.shape[1] - 1
    tap_reach = taps - 1
    rim_span = tap_reach + rim_edge
    block_rows = min(row_count, max(128, row_count // 8))
    span_cols = block_rows + tap_reach
    grad_scale = 1.0 / math.sqrt(row_count * lax.axis_size("ctx"))
    doc_marks = doc_ids + 1
    previous = shifted(
        (
            q_in[row_count - rim_edge :],
            k_in[row_count - rim_span :],
            v_in[row_count - rim_span :],
            doc_marks[row_count - rim_span :],
        ),
        "ctx",
        1,
    )
    marks_ext = jnp.concatenate([previous[3], doc_marks], axis=0)
    long_marks = marks_ext[rim_edge:]
    short_marks = marks_ext[tap_reach:]
    q_short = jnp.concatenate([previous[0], q_in], axis=0)
    k_ext = jnp.concatenate([previous[1], k_in], axis=0)
    v_ext = jnp.concatenate([previous[2], v_in], axis=0)
    k_short = k_ext[tap_reach:]
    v_short = v_ext[tap_reach:]
    k_wide = featurize(k_ext, short_weight[1], marks_ext, rim_edge)
    v_wide = featurize(v_ext, short_weight[2], marks_ext, rim_edge)
    product_ext = (k_wide * v_wide).astype(jnp.bfloat16)
    feat_k = k_wide[tap_reach:]
    feat_v = v_wide[tap_reach:]
    feat_q = featurize(q_short, short_weight[0], short_marks, rim_edge)
    forward_band = banded(filters[:, ::-1], block_rows)
    backward_band = banded(filters, block_rows)
    masks = []
    mixed_parts = []
    for start in range(0, row_count, block_rows):
        agree = (
            long_marks[start : start + span_cols][None, :]
            == doc_marks[start : start + block_rows][:, None]
        ).astype(jnp.bfloat16)
        masks.append(agree)
        segment = product_ext[start : start + span_cols].reshape(span_cols, groups, group_width)
        mixed_parts.append(
            jnp.einsum(
                "gij,jgc->igc",
                forward_band * agree[None],
                segment,
                preferred_element_type=jnp.float32,
            ).reshape(block_rows, channels)
        )
    mixed = jnp.concatenate(mixed_parts, axis=0)
    y_out = feat_q * mixed
    weighted = gain.astype(jnp.float32)[None, :] * grad_out.astype(jnp.float32)
    square_sum, inner_sum = lax.psum(
        (jnp.sum(y_out * y_out, axis=1), jnp.sum(weighted * y_out, axis=1)), "tp"
    )
    row_scale = lax.rsqrt(square_sum / D + EPS)
    grad_y = row_scale[:, None] * weighted - y_out * (row_scale**3 * inner_sum / D)[:, None]
    gain_term = (
        jnp.sum(grad_out.astype(jnp.float32) * y_out * row_scale[:, None], axis=0) * grad_scale
    )
    grad_gain = lax.psum(gain_term, "ctx")
    grad_fq = grad_y * mixed
    grad_mixed = (grad_y * feat_q).astype(jnp.bfloat16)
    following = shifted((grad_mixed[:tap_reach], doc_marks[:tap_reach]), "ctx", -1)
    mixed_ext = jnp.concatenate([grad_mixed, following[0]], axis=0)
    marks_after = jnp.concatenate([doc_marks, following[1]], axis=0)
    prod_parts = []
    filter_term = jnp.zeros((groups, taps), jnp.float32)
    for position, start in enumerate(range(0, row_count, block_rows)):
        agree = (
            marks_after[start : start + span_cols][None, :]
            == doc_marks[start : start + block_rows][:, None]
        ).astype(jnp.bfloat16)
        segment = mixed_ext[start : start + span_cols].reshape(span_cols, groups, group_width)
        prod_parts.append(
            jnp.einsum(
                "gij,jgc->igc",
                backward_band * agree[None],
                segment,
                preferred_element_type=jnp.float32,
            ).reshape(block_rows, channels)
        )
        own_block = grad_mixed[start : start + block_rows].reshape(block_rows, groups, group_width)
        behind = product_ext[start : start + span_cols].reshape(span_cols, groups, group_width)
        pair_grad = (
            jnp.einsum("igc,jgc->gij", own_block, behind, preferred_element_type=jnp.float32)
            * masks[position].astype(jnp.float32)[None]
        )
        filter_term = filter_term + diagonal_sums(pair_grad, taps)
    filter_term = filter_term[:, ::-1] * grad_scale
    grad_filters = lax.psum(filter_term, "ctx")
    grad_prod = jnp.concatenate(prod_parts, axis=0)
    grad_fk = grad_prod * feat_v
    grad_fv = grad_prod * feat_k
    tails_after = shifted(
        jnp.stack([grad_fq[:rim_edge], grad_fk[:rim_edge], grad_fv[:rim_edge]]), "ctx", -1
    )
    grad_q = unfeature(grad_fq, tails_after[0], short_weight[0], marks_after, doc_marks)
    grad_k = unfeature(grad_fk, tails_after[1], short_weight[1], marks_after, doc_marks)
    grad_v = unfeature(grad_fv, tails_after[2], short_weight[2], marks_after, doc_marks)
    short_term = (
        jnp.stack(
            [
                short_terms(grad_fq, q_short, short_marks, doc_marks, rim_edge),
                short_terms(grad_fk, k_short, short_marks, doc_marks, rim_edge),
                short_terms(grad_fv, v_short, short_marks, doc_marks, rim_edge),
            ]
        )
        * grad_scale
    )
    grad_short = lax.psum(short_term, "ctx")
    return (grad_q, grad_k, grad_v, grad_gain, grad_filters, grad_short)


def solution(mesh):
    return jax.shard_map(
        on_device,
        mesh=mesh,
        in_specs=(
            P("ctx", "tp"),
            P("ctx", "tp"),
            P("ctx", "tp"),
            P("ctx", "tp"),
            P("ctx"),
            P("tp"),
            P("tp", None),
            P(None, None, "tp"),
        ),
        out_specs=(
            P("ctx", "tp"),
            P("ctx", "tp"),
            P("ctx", "tp"),
            P("tp"),
            P("tp", None),
            P(None, None, "tp"),
        ),
        check_vma=False,
    )
```

profile of v0, /device:TPU:2, one launch (start us, length us, event | category | flops | bytes accessed | tf_op | source)
XLA Modules:
  0.0 352.5 jit_solution(16350759475145604191)
XLA Ops:
  8.2 3.8 %collective-permute-start.3 = (bf16[129,1024]{1,0:T(8,128)(2,1)S(1)}, bf16[129,1024]{1,0:T(8,128)(2,1)S(1)}, u32[]{:S(2)}, u32[]{:S(2)}) collective-permute-start(bf16[129,1024]{1,0:T(8,128)(2,1)S(1)} %slice.289), channel_id=1, source_target_pairs={{0,8},{8,16},{16,24},{24,32},{32,40},{40,48},{48,56},{56,64},{64,7... | collective-permute-start | bytes 792584 | tf_op jit(solution)/shard_map/ppermute | solution.py:14
  12.8 1.3 collective-permute-start.5
  14.1 4.5 %collective-permute-start.1 = (s32[129]{0:T(256)S(1)}, s32[129]{0:T(256)S(1)}, u32[]{:S(2)}, u32[]{:S(2)}) collective-permute-start(s32[129]{0:T(256)S(1)} %slice.273), channel_id=1, source_target_pairs={{0,8},{8,16},{16,24},{24,32},{32,40},{40,48},{48,56},{56,64},{64,7... | collective-permute-start | bytes 1556 | tf_op jit(solution)/shard_map/ppermute | solution.py:14
  18.7 1.3 slice.271
  20.0 4.4 %collective-permute-start = (bf16[2,1024]{1,0:T(2,128)(2,1)}, bf16[2,1024]{1,0:T(2,128)(2,1)}, u32[]{:S(2)}, u32[]{:S(2)}) collective-permute-start(bf16[2,1024]{1,0:T(2,128)(2,1)} %slice.271), channel_id=1, source_target_pairs={{0,8},{8,16},{16,24},{24,32},{32,40},{40,48},{48,56},{56,64},{64,7... | collective-permute-start | bytes 12296 | tf_op jit(solution)/shard_map/ppermute | solution.py:14
  25.4 4.4 %collective-permute-start.2 = (bf16[129,1024]{1,0:T(8,128)(2,1)S(1)}, bf16[129,1024]{1,0:T(8,128)(2,1)S(1)}, u32[]{:S(2)}, u32[]{:S(2)}) collective-permute-start(bf16[129,1024]{1,0:T(8,128)(2,1)S(1)} %slice.279), channel_id=1, source_target_pairs={{0,8},{8,16},{16,24},{24,32},{32,40},{40,48},{48,56},{56,64},{64,7... | collective-permute-start | bytes 792584 | tf_op jit(solution)/shard_map/ppermute | solution.py:14
  29.9 1.5 slice_convert_fusion.8
  33.2 2.6 copy.34
  35.8 2.3 slice.348
  38.1 16.1 %reshape.317 = bf16[64,128,255]{2,1,0:T(8,128)(2,1)} reshape(bf16[64,32640]{1,0:T(8,128)(2,1)} %slice.348) | data formatting | bytes 8355840 | tf_op jit(solution)/shard_map/reshape | solution.py:40
  55.1 2.6 copy.35
  57.7 2.3 slice.352
  60.0 15.9 %reshape.322 = bf16[64,128,255]{2,1,0:T(8,128)(2,1)} reshape(bf16[64,32640]{1,0:T(8,128)(2,1)} %slice.352) | data formatting | bytes 8355840 | tf_op jit(solution)/shard_map/reshape | solution.py:40
  77.7 5.0 %multiply_convert_fusion = (bf16[383,1024]{1,0:T(8,128)(2,1)S(1)}, f32[383,1024]{1,0:T(8,128)}, f32[383,1024]{1,0:T(8,128)}) fusion(f32[383]{0:T(512)S(1)} %get-tuple-element.56, f32[1024]{0:T(1024)S(1)} %bitcast.107, f32[383]{0:T(512)S(1)} %get-tuple-element.55, f32[1024]{0:T(1024)S(1)} %bitcast.109, bf16[256,1024]{1,0:T(8,128)(2,1)S(1)} %copy-done.13, ...), kind=kLoop, calls=%fused_computation.16 | loop fusion | flops 15687680 | bytes 5526520 | tf_op jit(solution)/shard_map/convert_element_type | solution.py:113
  83.3 3.6 %fusion.4 = f32[64,16,128]{2,1,0:T(8,128)S(1)} fusion(bf16[255,64,16]{0,2,1:T(8,128)(2,1)S(1)} %bitcast.78, bf16[64,128,255]{2,1,0:T(8,128)(2,1)} %reshape.317, bf16[128,255]{1,0:T(8,128)(2,1)S(1)} %get-tuple-element.70), kind=kOutput, calls=%fused_computation.8 | convolution fusion | flops 68935680 | bytes 5289728 | tf_op jit(solution)/shard_map/gij,jgc->igc/dot_general | solution.py:129
  86.9 1.2 fusion.6
  89.2 2.0 multiply_reduce_fusion.6
  91.2 10.7 %psum.35 = f32[256]{0:T(256)S(1)} all-reduce(f32[256]{0:T(256)} %get-tuple-element.26), channel_id=1, replica_groups=mesh['ctx'=32,'tp'=8] {'tp'}, use_global_device_ids=true, to_apply=%region_1.0 | all-reduce | flops 256 | bytes 2048 | tf_op jit(solution)/shard_map/psum | solution.py:139
  101.8 1.6 fusion.44
  103.5 12.4 %psum.36 = f32[256]{0:T(256)S(1)} all-reduce(f32[256]{0:T(256)S(1)} %get-tuple-element.16), channel_id=1, replica_groups=mesh['ctx'=32,'tp'=8] {'tp'}, use_global_device_ids=true, to_apply=%region_3.0 | all-reduce | flops 256 | bytes 2048 | tf_op jit(solution)/shard_map/psum | solution.py:139
  116.4 1.4 multiply_convert_fusion.1
  119.5 1.3 collective-permute-start.4
  120.8 1.8 copy.32
  122.6 5.5 %broadcast_multiply_fusion.1 = f32[64,128,255]{2,1,0:T(8,128)} fusion(f32[128,255]{1,0:T(8,128)} %get-tuple-element.59, bf16[128,64,16]{0,2,1:T(8,128)(2,1)} %bitcast.88, bf16[255,64,16]{0,2,1:T(8,128)(2,1)S(1)} %bitcast.81), kind=kOutput, calls=%fused_computation.3 | convolution fusion | flops 68935680 | bytes 9270784 | tf_op jit(solution)/shard_map/igc,jgc->gij/dot_general | solution.py:172
  128.1 9.4 %reshape.327 = f32[64,32640]{1,0:T(8,128)} reshape(f32[64,128,255]{2,1,0:T(8,128)} %broadcast_multiply_fusion.1) | data formatting | bytes 16711680 | tf_op jit(solution)/shard_map/reshape | solution.py:45
  137.5 4.0 %concatenate.58 = f32[64,32768]{1,0:T(8,128)S(1)} pad(f32[64,32640]{1,0:T(8,128)} %reshape.327, f32[]{:T(128)} %constant.19.clone.1), padding=0_0x0_128 | pad | bytes 16744452 | tf_op jit(solution)/shard_map/concatenate | solution.py:46
  141.6 2.5 copy.36
  144.1 1.1 slice_reduce_fusion.1
  145.2 1.8 copy.33
  147.0 5.5 %broadcast_multiply_fusion = f32[64,128,255]{2,1,0:T(8,128)} fusion(f32[128,255]{1,0:T(8,128)S(1)} %get-tuple-element.71, bf16[128,64,16]{0,2,1:T(8,128)(2,1)} %bitcast.89, bf16[255,64,16]{0,2,1:T(8,128)(2,1)S(1)} %bitcast.79), kind=kOutput, calls=%fused_computation.2 | convolution fusion | flops 68935680 | bytes 9270784 | tf_op jit(solution)/shard_map/igc,jgc->gij/dot_general | solution.py:172
  152.5 9.4 %reshape.330 = f32[64,32640]{1,0:T(8,128)} reshape(f32[64,128,255]{2,1,0:T(8,128)} %broadcast_multiply_fusion) | data formatting | bytes 16711680 | tf_op jit(solution)/shard_map/reshape | solution.py:45
  162.0 4.0 %concatenate.59 = f32[64,32768]{1,0:T(8,128)S(1)} pad(f32[64,32640]{1,0:T(8,128)} %reshape.330, f32[]{:T(128)} %constant.19.clone.1), padding=0_0x0_128 | pad | bytes 16744452 | tf_op jit(solution)/shard_map/concatenate | solution.py:46
  166.0 2.5 copy.37
  170.5 1.9 fusion.72
  172.4 1.2 copy.29
  173.7 4.2 %fusion = f32[64,16,128]{2,1,0:T(8,128)} fusion(bf16[255,64,16]{0,2,1:T(8,128)(2,1)S(1)} %bitcast.86, bf16[64,128,255]{2,1,0:T(8,128)(2,1)} %reshape.322, bf16[128,255]{1,0:T(8,128)(2,1)S(1)} %copy-done.19), kind=kOutput, calls=%fused_computation.4 | convolution fusion | flops 68935680 | bytes 5289728 | tf_op jit(solution)/shard_map/gij,jgc->igc/dot_general | solution.py:162
  177.9 1.3 copy.31
  180.2 4.4 %fusion.2 = f32[64,16,128]{2,1,0:T(8,128)} fusion(bf16[255,64,16]{0,2,1:T(8,128)(2,1)} %bitcast.84, bf16[64,128,255]{2,1,0:T(8,128)(2,1)} %reshape.322, bf16[128,255]{1,0:T(8,128)(2,1)S(1)} %copy-done.18), kind=kOutput, calls=%fused_computation.6 | convolution fusion | flops 68935680 | bytes 5289728 | tf_op jit(solution)/shard_map/gij,jgc->igc/dot_general | solution.py:162
  184.5 1.2 copy.30
  185.9 4.1 %multiply_reduce_fusion.1 = (f32[1024]{0:T(1024)S(1)}, f32[1024]{0:T(1024)S(1)}, f32[1024]{0:T(1024)S(1)}, f32[1024]{0:T(1024)S(1)}, f32[1024]{0:T(1024)S(1)}, /...) fusion(bf16[256,1024]{1,0:T(8,128)(2,1)} %param.10, ...), kind=kLoop, calls=%fused_computation.88 | loop fusion | flops 11266048 | bytes 8165376 | tf_op jit(solution)/shard_map/reduce_sum | solution.py:74
  191.3 1.3 collective-permute-start.6
  193.3 5.2 %collective-permute-done.6 = f32[3,2,1024]{2,1,0:T(2,128)S(1)} collective-permute-done((f32[3,2,1024]{2,1,0:T(2,128)S(1)}, f32[3,2,1024]{2,1,0:T(2,128)S(1)}, u32[]{:S(2)}, u32[]{:S(2)}) %collective-permute-start.6) | collective-permute-done | bytes 24608 | tf_op jit(solution)/shard_map/ppermute | solution.py:14
  198.7 4.0 %fusion.19 = (bf16[256,1024]{1,0:T(8,128)(2,1)}, bf16[256,1024]{1,0:T(8,128)(2,1)}) fusion(f32[256,1024]{1,0:T(8,128)} %copy-done.12, f32[2,1024]{1,0:T(2,128)S(1)} %get-tuple-element.37, f32[1024]{0:T(1024)S(1)} %bitcast.108, f32[1024]{0:T(1024)S(1)} %bitcast.110, f32[1024]{0:T(1024)S(1)} %bitcast.100, f32[256]{0:T(256)S(1)} %copy-done.45, ...), kind=kLoop, calls=%fused_computation.48 | loop fusion | flops 5242880 | bytes 3188736 | tf_op jit(solution)/shard_map/convert_element_type | solution.py:62
  202.7 1.2 fusion.31
  203.9 137.5 %all-reduce.7.cloned.1.call-done = (f32[1024]{0:T(1024)}, f32[64,128]{1,0:T(8,128)}, f32[3,3,1024]{2,1,0:T(4,128)}) async-done(((f32[1024]{0:T(1024)}, f32[64,128]{1,0:T(8,128)}, f32[3,3,1024]{2,1,0:T(4,128)}), (f32[1024]{0:T(1024)}, f32[64,128]{1,0:T(8,128)}, f32[3,3,1024]{2,1,0:T(4,128)})) %all-reduce.7.cloned.1.call-update) | async-done | bytes 73744 | tf_op jit(solution)/shard_map/psum | solution.py:147
  341.4 1.3 copy.41
  342.6 1.4 copy.42
  344.0 1.4 copy.43
  (149 shorter events, 16.1 us)
Async XLA Ops:
  7.2 334.2 %all-reduce.7.cloned.1.call-start = ((), (), s32[]{:S(2)}) async-start(), calls=%async_computation | async-start | bytes 172032 | tf_op jit(solution)/shard_map/psum | solution.py:147
  8.2 69.4 %collective-permute-start.3 = (bf16[129,1024]{1,0:T(8,128)(2,1)S(1)}, bf16[129,1024]{1,0:T(8,128)(2,1)S(1)}, u32[]{:S(2)}, u32[]{:S(2)}) collective-permute-start(bf16[129,1024]{1,0:T(8,128)(2,1)S(1)} %slice.289), channel_id=1, source_target_pairs={{0,8},{8,16},{16,24},{24,32},{32,40},{40,48},{48,56},{56,64},{64,7... | collective-permute-start | bytes 792584 | tf_op jit(solution)/shard_map/ppermute | solution.py:14
  12.8 63.1 %collective-permute-start.5 = (s32[127]{0:T(128)S(1)}, s32[127]{0:T(128)S(1)}, u32[]{:S(2)}, u32[]{:S(2)}) collective-permute-start(s32[127]{0:T(128)S(1)} %slice.308), channel_id=1, source_target_pairs={{8,0},{16,8},{24,16},{32,24},{40,32},{48,40},{56,48},{64,56},{72,6... | collective-permute-start | bytes 1532 | tf_op jit(solution)/shard_map/ppermute | solution.py:14
  14.1 61.7 %collective-permute-start.1 = (s32[129]{0:T(256)S(1)}, s32[129]{0:T(256)S(1)}, u32[]{:S(2)}, u32[]{:S(2)}) collective-permute-start(s32[129]{0:T(256)S(1)} %slice.273), channel_id=1, source_target_pairs={{0,8},{8,16},{16,24},{24,32},{32,40},{40,48},{48,56},{56,64},{64,7... | collective-permute-start | bytes 1556 | tf_op jit(solution)/shard_map/ppermute | solution.py:14
  20.0 68.6 %collective-permute-start = (bf16[2,1024]{1,0:T(2,128)(2,1)}, bf16[2,1024]{1,0:T(2,128)(2,1)}, u32[]{:S(2)}, u32[]{:S(2)}) collective-permute-start(bf16[2,1024]{1,0:T(2,128)(2,1)} %slice.271), channel_id=1, source_target_pairs={{0,8},{8,16},{16,24},{24,32},{32,40},{40,48},{48,56},{56,64},{64,7... | collective-permute-start | bytes 12296 | tf_op jit(solution)/shard_map/ppermute | solution.py:14
  25.4 52.2 %collective-permute-start.2 = (bf16[129,1024]{1,0:T(8,128)(2,1)S(1)}, bf16[129,1024]{1,0:T(8,128)(2,1)S(1)}, u32[]{:S(2)}, u32[]{:S(2)}) collective-permute-start(bf16[129,1024]{1,0:T(8,128)(2,1)S(1)} %slice.279), channel_id=1, source_target_pairs={{0,8},{8,16},{16,24},{24,32},{32,40},{40,48},{48,56},{56,64},{64,7... | collective-permute-start | bytes 792584 | tf_op jit(solution)/shard_map/ppermute | solution.py:14
  31.4 46.2 %copy-start.25 = (f32[1,1,1024]{2,1,0:T(1,128)}, f32[1,1,1024]{2,1,0:T(1,128)S(1)}, u32[]{:S(2)}) copy-start(f32[1,1,1024]{2,1,0:T(1,128)S(1)} %get-tuple-element.41) | copy-start | bytes 12292
  31.4 46.2 %copy-start.27 = (f32[1,1,1024]{2,1,0:T(1,128)}, f32[1,1,1024]{2,1,0:T(1,128)S(1)}, u32[]{:S(2)}) copy-start(f32[1,1,1024]{2,1,0:T(1,128)S(1)} %get-tuple-element.42) | copy-start | bytes 12292
  31.4 46.2 %copy-start.29 = (f32[1,1,1024]{2,1,0:T(1,128)}, f32[1,1,1024]{2,1,0:T(1,128)S(1)}, u32[]{:S(2)}) copy-start(f32[1,1,1024]{2,1,0:T(1,128)S(1)} %get-tuple-element.43) | copy-start | bytes 12292
  31.4 46.2 %copy-start.31 = (f32[1,1,1024]{2,1,0:T(1,128)}, f32[1,1,1024]{2,1,0:T(1,128)S(1)}, u32[]{:S(2)}) copy-start(f32[1,1,1024]{2,1,0:T(1,128)S(1)} %get-tuple-element.44) | copy-start | bytes 12292
  31.4 46.2 %copy-start.33 = (f32[1,1,1024]{2,1,0:T(1,128)}, f32[1,1,1024]{2,1,0:T(1,128)S(1)}, u32[]{:S(2)}) copy-start(f32[1,1,1024]{2,1,0:T(1,128)S(1)} %get-tuple-element.47) | copy-start | bytes 12292
  31.4 46.2 %copy-start.35 = (f32[1,1,1024]{2,1,0:T(1,128)}, f32[1,1,1024]{2,1,0:T(1,128)S(1)}, u32[]{:S(2)}) copy-start(f32[1,1,1024]{2,1,0:T(1,128)S(1)} %get-tuple-element.48) | copy-start | bytes 12292
  38.1 16.1 %copy-start.47 = (bf16[1024]{0:T(1024)(128)(2,1)S(1)}, bf16[1024]{0:T(1024)(128)(2,1)}, u32[]{:S(2)}) copy-start(bf16[1024]{0:T(1024)(128)(2,1)} %param.13) | copy-start | bytes 6148
  60.0 16.0 %copy-start.46 = (s32[256]{0:T(256)S(1)}, s32[256]{0:T(256)}, u32[]{:S(2)}) copy-start(s32[256]{0:T(256)} %param.12) | copy-start | bytes 3076
  60.0 17.7 %copy-start.13 = (bf16[256,1024]{1,0:T(8,128)(2,1)S(1)}, bf16[256,1024]{1,0:T(8,128)(2,1)}, u32[]{:S(2)}) copy-start(bf16[256,1024]{1,0:T(8,128)(2,1)} %param.10) | copy-start | bytes 1572868
  60.0 17.7 %copy-start.14 = (bf16[256,1024]{1,0:T(8,128)(2,1)S(1)}, bf16[256,1024]{1,0:T(8,128)(2,1)}, u32[]{:S(2)}) copy-start(bf16[256,1024]{1,0:T(8,128)(2,1)} %param.9) | copy-start | bytes 1572868
  77.6 5.1 %copy-start.16 = (bf16[129,1024]{1,0:T(8,128)(2,1)}, bf16[129,1024]{1,0:T(8,128)(2,1)S(1)}, u32[]{:S(2)}) copy-start(bf16[129,1024]{1,0:T(8,128)(2,1)S(1)} %collective-permute-done.2) | copy-start | bytes 792580
  83.0 3.8 %copy-start.5 = (bf16[255,1024]{0,1:T(8,128)(2,1)}, bf16[255,1024]{0,1:T(8,128)(2,1)S(1)}, u32[]{:S(2)}) copy-start(bf16[255,1024]{0,1:T(8,128)(2,1)S(1)} %copy.25) | copy-start | bytes 1566724
  83.2 3.6 %copy-start.7 = (bf16[255,1024]{0,1:T(8,128)(2,1)}, bf16[255,1024]{0,1:T(8,128)(2,1)S(1)}, u32[]{:S(2)}) copy-start(bf16[255,1024]{0,1:T(8,128)(2,1)S(1)} %copy.24) | copy-start | bytes 1566724
  83.2 3.6 %copy-start = (bf16[64,128,255]{2,1,0:T(8,128)(2,1)S(1)}, bf16[64,128,255]{2,1,0:T(8,128)(2,1)}, u32[]{:S(2)}) copy-start(bf16[64,128,255]{2,1,0:T(8,128)(2,1)} %reshape.317) | copy-start | bytes 12533764
  88.5 14.9 %copy-start.4 = (f32[128,1024]{1,0:T(8,128)}, f32[128,1024]{1,0:T(8,128)S(1)}, u32[]{:S(2)}) copy-start(f32[128,1024]{1,0:T(8,128)S(1)} %copy.26) | copy-start | bytes 1572868
  88.5 13.3 %copy-start.2 = (bf16[256,1024]{1,0:T(8,128)(2,1)S(1)}, bf16[256,1024]{1,0:T(8,128)(2,1)}, u32[]{:S(2)}) copy-start(bf16[256,1024]{1,0:T(8,128)(2,1)} %param.11) | copy-start | bytes 1572868
  101.8 14.0 %copy-start.39 = (f32[256]{0:T(256)}, f32[256]{0:T(256)S(1)}, u32[]{:S(2)}) copy-start(f32[256]{0:T(256)S(1)} %add_rsqrt_fusion) | copy-start | bytes 3076
  117.9 4.7 %copy-start.8 = (bf16[255,1024]{0,1:T(8,128)(2,1)S(1)}, bf16[255,1024]{0,1:T(8,128)(2,1)}, u32[]{:S(2)}) copy-start(bf16[255,1024]{0,1:T(8,128)(2,1)} %copy-done.7) | copy-start | bytes 1566724
  119.5 51.0 %collective-permute-start.4 = (bf16[127,1024]{1,0:T(8,128)(2,1)}, bf16[127,1024]{1,0:T(8,128)(2,1)}, u32[]{:S(2)}, u32[]{:S(2)}) collective-permute-start(bf16[127,1024]{1,0:T(8,128)(2,1)} %slice.353), channel_id=1, source_target_pairs={{8,0},{16,8},{24,16},{32,24},{40,32},{48,40},{56,48},{64,56},{72,6... | collective-permute-start | bytes 780296 | tf_op jit(solution)/shard_map/ppermute | solution.py:14
  144.1 2.9 copy-start.6
  170.5 3.2 copy-start.19
  180.1 5.6 %copy-start.21 = (f32[1024]{0:T(1024)S(1)}, f32[1024]{0:T(1024)}, u32[]{:S(2)}) copy-start(f32[1024]{0:T(1024)} %convert_element_type.293) | copy-start | bytes 12292
  180.1 5.6 %copy-start.37 = (f32[256]{0:T(256)S(1)}, f32[256]{0:T(256)}, u32[]{:S(2)}) copy-start(f32[256]{0:T(256)} %get-tuple-element.61) | copy-start | bytes 3076
  180.1 5.6 %copy-start.38 = (f32[256]{0:T(256)S(1)}, f32[256]{0:T(256)}, u32[]{:S(2)}) copy-start(f32[256]{0:T(256)} %get-tuple-element.62) | copy-start | bytes 3076
  180.2 5.6 %copy-start.40 = (f32[256]{0:T(256)S(1)}, f32[256]{0:T(256)}, u32[]{:S(2)}) copy-start(f32[256]{0:T(256)} %copy-done.39) | copy-start | bytes 3076
  180.2 5.6 %copy-start.43 = (f32[256]{0:T(256)S(1)}, f32[256]{0:T(256)}, u32[]{:S(2)}) copy-start(f32[256]{0:T(256)} %copy-done.42) | copy-start | bytes 3076
  185.8 4.2 %copy-start.9 = (f32[383,1024]{1,0:T(8,128)S(1)}, f32[383,1024]{1,0:T(8,128)}, u32[]{:S(2)}) copy-start(f32[383,1024]{1,0:T(8,128)} %get-tuple-element.29) | copy-start | bytes 4706308
  185.8 4.2 %copy-start.15 = (bf16[256,1024]{1,0:T(8,128)(2,1)S(1)}, bf16[256,1024]{1,0:T(8,128)(2,1)}, u32[]{:S(2)}) copy-start(bf16[256,1024]{1,0:T(8,128)(2,1)} %param.9) | copy-start | bytes 1572868
  185.8 4.2 %copy-start.17 = (bf16[129,1024]{1,0:T(8,128)(2,1)S(1)}, bf16[129,1024]{1,0:T(8,128)(2,1)}, u32[]{:S(2)}) copy-start(bf16[129,1024]{1,0:T(8,128)(2,1)} %copy-done.16) | copy-start | bytes 792580
  190.0 8.6 %copy-start.26 = (f32[1,1,1024]{2,1,0:T(1,128)S(1)}, f32[1,1,1024]{2,1,0:T(1,128)}, u32[]{:S(2)}) copy-start(f32[1,1,1024]{2,1,0:T(1,128)} %copy-done.25) | copy-start | bytes 12292
  190.0 8.5 %copy-start.28 = (f32[1,1,1024]{2,1,0:T(1,128)S(1)}, f32[1,1,1024]{2,1,0:T(1,128)}, u32[]{:S(2)}) copy-start(f32[1,1,1024]{2,1,0:T(1,128)} %copy-done.27) | copy-start | bytes 12292
  190.0 8.5 %copy-start.30 = (f32[1,1,1024]{2,1,0:T(1,128)S(1)}, f32[1,1,1024]{2,1,0:T(1,128)}, u32[]{:S(2)}) copy-start(f32[1,1,1024]{2,1,0:T(1,128)} %copy-done.29) | copy-start | bytes 12292
  190.0 8.5 %copy-start.32 = (f32[1,1,1024]{2,1,0:T(1,128)S(1)}, f32[1,1,1024]{2,1,0:T(1,128)}, u32[]{:S(2)}) copy-start(f32[1,1,1024]{2,1,0:T(1,128)} %copy-done.31) | copy-start | bytes 12292
  190.1 8.5 %copy-start.34 = (f32[1,1,1024]{2,1,0:T(1,128)S(1)}, f32[1,1,1024]{2,1,0:T(1,128)}, u32[]{:S(2)}) copy-start(f32[1,1,1024]{2,1,0:T(1,128)} %copy-done.33) | copy-start | bytes 12292
  190.1 8.5 %copy-start.36 = (f32[1,1,1024]{2,1,0:T(1,128)S(1)}, f32[1,1,1024]{2,1,0:T(1,128)}, u32[]{:S(2)}) copy-start(f32[1,1,1024]{2,1,0:T(1,128)} %copy-done.35) | copy-start | bytes 12292
  190.1 8.5 %copy-start.44 = (f32[256]{0:T(256)S(1)}, f32[256]{0:T(256)}, u32[]{:S(2)}) copy-start(f32[256]{0:T(256)} %get-tuple-element.49) | copy-start | bytes 3076
  190.1 8.5 %copy-start.45 = (f32[256]{0:T(256)S(1)}, f32[256]{0:T(256)}, u32[]{:S(2)}) copy-start(f32[256]{0:T(256)} %get-tuple-element.50) | copy-start | bytes 3076
  191.3 7.3 %collective-permute-start.6 = (f32[3,2,1024]{2,1,0:T(2,128)S(1)}, f32[3,2,1024]{2,1,0:T(2,128)S(1)}, u32[]{:S(2)}, u32[]{:S(2)}) collective-permute-start(f32[3,2,1024]{2,1,0:T(2,128)S(1)} %pad_maximum_fusion.9), channel_id=1, source_target_pairs={{8,0},{16,8},{24,16},{32,24},{40,32},{48,40},{56,48},{64,56},{72,6... | collective-permute-start | bytes 73736 | tf_op jit(solution)/shard_map/ppermute | solution.py:14
  198.6 4.0 %copy-start.11 = (f32[256,1024]{1,0:T(8,128)S(1)}, f32[256,1024]{1,0:T(8,128)}, u32[]{:S(2)}) copy-start(f32[256,1024]{1,0:T(8,128)} %copy-done.10) | copy-start | bytes 3145732
  198.6 4.0 %copy-start.22 = (f32[1,1,1024]{2,1,0:T(1,128)S(1)}, f32[1,1,1024]{2,1,0:T(1,128)}, u32[]{:S(2)}) copy-start(f32[1,1,1024]{2,1,0:T(1,128)} %get-tuple-element.40) | copy-start | bytes 12292
  198.6 4.0 %copy-start.23 = (f32[1,1,1024]{2,1,0:T(1,128)S(1)}, f32[1,1,1024]{2,1,0:T(1,128)}, u32[]{:S(2)}) copy-start(f32[1,1,1024]{2,1,0:T(1,128)} %get-tuple-element.45) | copy-start | bytes 12292
  198.7 4.0 %copy-start.24 = (f32[1,1,1024]{2,1,0:T(1,128)S(1)}, f32[1,1,1024]{2,1,0:T(1,128)}, u32[]{:S(2)}) copy-start(f32[1,1,1024]{2,1,0:T(1,128)} %get-tuple-element.46) | copy-start | bytes 12292
  (8 other events, 11.0 us)
Sparse Core Ops, SparseCore 0:
  193.5 147.8 all-reduce.6
where the time goes:
time: 357 us; the launch traced here: 353 us
  waiting for transfers between devices  143 us (40%)
  local copies, waits for them, and re-layouts  96.4 us (27%)
  other arithmetic  29.8 us (8%)
  matrix products  24.4 us (7%)
  blocking collectives  23.1 us (6%)
  starting transfers between devices  21 us (6%)
  between operations  15.1 us (4%)
    psum x1, waiting for transfers between devices, on_device(): grad_gain = lax.psum(gain_term, 'ctx')  137 us
    reshape x2, local copies, waits for them, and re-layouts, banded(): return repeated.reshape(groups, block_rows, span_cols)  32 us
    psum x2, blocking collectives, on_device(): lax.psum((jnp.sum(y_out * y_out, axis=1), jnp.sum(weighted * y_out, axis=...  23.1 us
    ppermute x7, starting transfers between devices, shifted(): return lax.ppermute(value, axis, pairs)  21 us
    reshape x2, local copies, waits for them, and re-layouts, diagonal_sums(): flat_terms = pair_grad.reshape(groups, block_rows * span_cols)  18.8 us
    unnamed x103, local copies, waits for them, and re-layouts  16.4 us
    dot_general x2, matrix products, on_device(): jnp.einsum('igc,jgc->gij', own_block, behind, preferred_element_type=jnp....  11 us
    dot_general x2, matrix products, on_device(): jnp.einsum('gij,jgc->igc', backward_band * agree[None], segment, preferre...  8.53 us
  transfers between devices with their start and end apart: 8, of which 2 were waited for; matrix products, arithmetic and copies ran while one was open for 33% of the time, Pallas kernels for 0%

commit v1 on v0

--- a/solution.py
+++ b/solution.py
@@ -144,7 +144,11 @@
     gain_term = (
         jnp.sum(grad_out.astype(jnp.float32) * y_out * row_scale[:, None], axis=0) * grad_scale
     )
-    grad_gain = lax.psum(gain_term, "ctx")
+    grad_gain = gain_term
+    for hop in (1, 2, 4, 8, 16):
+        grad_gain = grad_gain + lax.ppermute(
+            grad_gain, "ctx", [(dev, dev ^ hop) for dev in range(32)]
+        )
     grad_fq = grad_y * mixed
     grad_mixed = (grad_y * feat_q).astype(jnp.bfloat16)
     following = shifted((grad_mixed[:tap_reach], doc_marks[:tap_reach]), "ctx", -1)

time: 357 us -> 369 us (1.034)
  starting transfers between devices: 21 us -> 33.9 us
    ppermute x0 -> x5, starting transfers between devices: none -> 12.9 us  [on_device(): lax.ppermute(grad_gain, 'ctx', [(dev, dev ^ hop) for dev in range(32)])]
    unnamed x103 -> x98, local copies, waits for them, and re-layouts: 16.4 us -> 14.4 us
  transfers between devices with their start and end apart: 8 -> 13, of which waited for: 2 -> 4; matrix products, arithmetic and copies ran while one was open for 33% -> 32% of each run, Pallas kernels for 0% -> 0%
where the time goes in v1:
time: 369 us; the launch traced here: 365 us
  waiting for transfers between devices  143 us (39%)
  local copies, waits for them, and re-layouts  93.4 us (25%)
  starting transfers between devices  33.9 us (9%)
  other arithmetic  31.7 us (9%)
  matrix products  24.6 us (7%)
  blocking collectives  23.1 us (6%)
  between operations  15.1 us (4%)
    psum x1, waiting for transfers between devices, on_device(): grad_filters = lax.psum(filter_term, 'ctx')  136 us
    reshape x2, local copies, waits for them, and re-layouts, banded(): return repeated.reshape(groups, block_rows, span_cols)  32 us
    psum x2, blocking collectives, on_device(): lax.psum((jnp.sum(y_out * y_out, axis=1), jnp.sum(weighted * y_out, axis=...  23.1 us
    ppermute x7, starting transfers between devices, shifted(): return lax.ppermute(value, axis, pairs)  21 us
    reshape x2, local copies, waits for them, and re-layouts, diagonal_sums(): flat_terms = pair_grad.reshape(groups, block_rows * span_cols)  18.8 us
    unnamed x98, local copies, waits for them, and re-layouts  14.4 us
    ppermute x5, starting transfers between devices, on_device(): lax.ppermute(grad_gain, 'ctx', [(dev, dev ^ hop) for dev in range(32)])  12.9 us
    dot_general x2, matrix products, on_device(): jnp.einsum('igc,jgc->gij', own_block, behind, preferred_element_type=jnp....  11.2 us
  transfers between devices with their start and end apart: 13, of which 4 were waited for; matrix products, arithmetic and copies ran while one was open for 32% of the time, Pallas kernels for 0%

profile of v1, /device:TPU:2, one launch (start us, length us, event | category | flops | bytes accessed | tf_op | source)
XLA Modules:
  0.0 364.5 jit_solution(7285351024216975432)
XLA Ops:
  8.2 3.8 %collective-permute-start.3 = (bf16[129,1024]{1,0:T(8,128)(2,1)S(1)}, bf16[129,1024]{1,0:T(8,128)(2,1)S(1)}, u32[]{:S(2)}, u32[]{:S(2)}) collective-permute-start(bf16[129,1024]{1,0:T(8,128)(2,1)S(1)} %slice.289), channel_id=1, source_target_pairs={{0,8},{8,16},{16,24},{24,32},{32,40},{40,48},{48,56},{56,64},{64,7... | collective-permute-start | bytes 792584 | tf_op jit(solution)/shard_map/ppermute | solution.py:14
  12.8 1.3 collective-permute-start.5
  14.1 4.5 %collective-permute-start.1 = (s32[129]{0:T(256)S(1)}, s32[129]{0:T(256)S(1)}, u32[]{:S(2)}, u32[]{:S(2)}) collective-permute-start(s32[129]{0:T(256)S(1)} %slice.273), channel_id=1, source_target_pairs={{0,8},{8,16},{16,24},{24,32},{32,40},{40,48},{48,56},{56,64},{64,7... | collective-permute-start | bytes 1556 | tf_op jit(solution)/shard_map/ppermute | solution.py:14
  18.7 1.3 slice.271
  20.0 4.4 %collective-permute-start = (bf16[2,1024]{1,0:T(2,128)(2,1)}, bf16[2,1024]{1,0:T(2,128)(2,1)}, u32[]{:S(2)}, u32[]{:S(2)}) collective-permute-start(bf16[2,1024]{1,0:T(2,128)(2,1)} %slice.271), channel_id=1, source_target_pairs={{0,8},{8,16},{16,24},{24,32},{32,40},{40,48},{48,56},{56,64},{64,7... | collective-permute-start | bytes 12296 | tf_op jit(solution)/shard_map/ppermute | solution.py:14
  25.4 4.4 %collective-permute-start.2 = (bf16[129,1024]{1,0:T(8,128)(2,1)S(1)}, bf16[129,1024]{1,0:T(8,128)(2,1)S(1)}, u32[]{:S(2)}, u32[]{:S(2)}) collective-permute-start(bf16[129,1024]{1,0:T(8,128)(2,1)S(1)} %slice.279), channel_id=1, source_target_pairs={{0,8},{8,16},{16,24},{24,32},{32,40},{40,48},{48,56},{56,64},{64,7... | collective-permute-start | bytes 792584 | tf_op jit(solution)/shard_map/ppermute | solution.py:14
  29.9 1.5 slice_convert_fusion.8
  33.2 2.6 copy.34
  35.8 2.3 slice.348
  38.1 16.1 %reshape.317 = bf16[64,128,255]{2,1,0:T(8,128)(2,1)} reshape(bf16[64,32640]{1,0:T(8,128)(2,1)} %slice.348) | data formatting | bytes 8355840 | tf_op jit(solution)/shard_map/reshape | solution.py:40
  55.1 2.6 copy.35
  57.7 2.3 slice.352
  60.0 15.9 %reshape.322 = bf16[64,128,255]{2,1,0:T(8,128)(2,1)} reshape(bf16[64,32640]{1,0:T(8,128)(2,1)} %slice.352) | data formatting | bytes 8355840 | tf_op jit(solution)/shard_map/reshape | solution.py:40
  77.7 4.9 %multiply_convert_fusion = (bf16[383,1024]{1,0:T(8,128)(2,1)S(1)}, f32[383,1024]{1,0:T(8,128)}, f32[383,1024]{1,0:T(8,128)}) fusion(f32[383]{0:T(512)S(1)} %get-tuple-element.55, f32[1024]{0:T(1024)S(1)} %bitcast.107, f32[383]{0:T(512)S(1)} %get-tuple-element.54, f32[1024]{0:T(1024)S(1)} %bitcast.109, bf16[256,1024]{1,0:T(8,128)(2,1)S(1)} %copy-done.12, ...), kind=kLoop, calls=%fused_computation.16 | loop fusion | flops 15687680 | bytes 5526520 | tf_op jit(solution)/shard_map/convert_element_type | solution.py:113
  83.2 3.6 fusion.4
  89.1 2.0 multiply_reduce_fusion.6
  91.1 10.7 %psum.28 = f32[256]{0:T(256)S(1)} all-reduce(f32[256]{0:T(256)} %get-tuple-element.25), channel_id=1, replica_groups=mesh['ctx'=32,'tp'=8] {'tp'}, use_global_device_ids=true, to_apply=%region_1.0 | all-reduce | flops 256 | bytes 2048 | tf_op jit(solution)/shard_map/psum | solution.py:139
  101.8 1.6 fusion.44
  103.4 12.4 %psum.29 = f32[256]{0:T(256)S(1)} all-reduce(f32[256]{0:T(256)S(1)} %get-tuple-element.16), channel_id=1, replica_groups=mesh['ctx'=32,'tp'=8] {'tp'}, use_global_device_ids=true, to_apply=%region_3.0 | all-reduce | flops 256 | bytes 2048 | tf_op jit(solution)/shard_map/psum | solution.py:139
  115.8 1.5 multiply_convert_fusion.1
  118.8 1.3 collective-permute-start.4
  120.7 3.6 collective-permute-start.7
  125.1 5.8 %broadcast_multiply_fusion.1 = f32[64,128,255]{2,1,0:T(8,128)} fusion(f32[128,255]{1,0:T(8,128)} %get-tuple-element.58, bf16[128,64,16]{0,2,1:T(8,128)(2,1)} %bitcast.89, bf16[255,64,16]{0,2,1:T(8,128)(2,1)} %bitcast.81), kind=kOutput, calls=%fused_computation.3 | convolution fusion | flops 68935680 | bytes 9270784 | tf_op jit(solution)/shard_map/igc,jgc->gij/dot_general | solution.py:176
  130.9 1.8 copy.33
  132.7 1.3 fusion.68
  134.0 1.7 collective-permute-start.8
  135.7 5.5 %broadcast_multiply_fusion = f32[64,128,255]{2,1,0:T(8,128)} fusion(f32[128,255]{1,0:T(8,128)S(1)} %get-tuple-element.70, bf16[128,64,16]{0,2,1:T(8,128)(2,1)} %bitcast.88, bf16[255,64,16]{0,2,1:T(8,128)(2,1)S(1)} %bitcast.79), kind=kOutput, calls=%fused_computation.2 | convolution fusion | flops 68935680 | bytes 9270784 | tf_op jit(solution)/shard_map/igc,jgc->gij/dot_general | solution.py:176
  141.2 9.5 %reshape.327 = f32[64,32640]{1,0:T(8,128)} reshape(f32[64,128,255]{2,1,0:T(8,128)} %broadcast_multiply_fusion.1) | data formatting | bytes 16711680 | tf_op jit(solution)/shard_map/reshape | solution.py:45
  150.6 4.0 %concatenate.58 = f32[64,32768]{1,0:T(8,128)S(1)} pad(f32[64,32640]{1,0:T(8,128)} %reshape.327, f32[]{:T(128)} %constant.19.clone.1), padding=0_0x0_128 | pad | bytes 16744452 | tf_op jit(solution)/shard_map/concatenate | solution.py:46
  154.7 2.5 copy.36
  157.9 2.6 collective-permute-start.9
  161.0 9.3 %reshape.330 = f32[64,32640]{1,0:T(8,128)} reshape(f32[64,128,255]{2,1,0:T(8,128)} %broadcast_multiply_fusion) | data formatting | bytes 16711680 | tf_op jit(solution)/shard_map/reshape | solution.py:45
  170.3 4.0 %concatenate.59 = f32[64,32768]{1,0:T(8,128)S(1)} pad(f32[64,32640]{1,0:T(8,128)} %reshape.330, f32[]{:T(128)} %constant.19.clone.1), padding=0_0x0_128 | pad | bytes 16744452 | tf_op jit(solution)/shard_map/concatenate | solution.py:46
  174.3 2.5 copy.37
  176.9 1.7 collective-permute-start.10
  179.1 1.4 collective-permute-done.10
  180.6 3.4 collective-permute-start.11
  184.6 1.3 collective-permute-done.11
  186.5 1.9 fusion.73
  189.6 4.2 %fusion = f32[64,16,128]{2,1,0:T(8,128)} fusion(bf16[255,64,16]{0,2,1:T(8,128)(2,1)S(1)} %bitcast.86, bf16[64,128,255]{2,1,0:T(8,128)(2,1)} %reshape.322, bf16[128,255]{1,0:T(8,128)(2,1)S(1)} %copy-done.18), kind=kOutput, calls=%fused_computation.4 | convolution fusion | flops 68935680 | bytes 5289728 | tf_op jit(solution)/shard_map/gij,jgc->igc/dot_general | solution.py:166
  196.1 4.4 %fusion.2 = f32[64,16,128]{2,1,0:T(8,128)} fusion(bf16[255,64,16]{0,2,1:T(8,128)(2,1)} %bitcast.84, bf16[64,128,255]{2,1,0:T(8,128)(2,1)} %reshape.322, bf16[128,255]{1,0:T(8,128)(2,1)S(1)} %copy-done.17), kind=kOutput, calls=%fused_computation.6 | convolution fusion | flops 68935680 | bytes 5289728 | tf_op jit(solution)/shard_map/gij,jgc->igc/dot_general | solution.py:166
  201.8 4.1 %multiply_reduce_fusion.1 = (f32[1024]{0:T(1024)S(1)}, f32[1024]{0:T(1024)S(1)}, f32[1024]{0:T(1024)S(1)}, f32[1024]{0:T(1024)S(1)}, f32[1024]{0:T(1024)S(1)}, /...) fusion(bf16[256,1024]{1,0:T(8,128)(2,1)} %param.10, ...), kind=kLoop, calls=%fused_computation.88 | loop fusion | flops 11266048 | bytes 8165376 | tf_op jit(solution)/shard_map/reduce_sum | solution.py:74
  207.2 1.3 collective-permute-start.6
  209.3 3.7 %collective-permute-done.6 = f32[3,2,1024]{2,1,0:T(2,128)S(1)} collective-permute-done((f32[3,2,1024]{2,1,0:T(2,128)S(1)}, f32[3,2,1024]{2,1,0:T(2,128)S(1)}, u32[]{:S(2)}, u32[]{:S(2)}) %collective-permute-start.6) | collective-permute-done | bytes 24608 | tf_op jit(solution)/shard_map/ppermute | solution.py:14
  213.1 3.9 %fusion.19 = (bf16[256,1024]{1,0:T(8,128)(2,1)}, bf16[256,1024]{1,0:T(8,128)(2,1)}) fusion(f32[256,1024]{1,0:T(8,128)} %copy-done.11, f32[2,1024]{1,0:T(2,128)S(1)} %get-tuple-element.36, f32[1024]{0:T(1024)S(1)} %bitcast.108, f32[1024]{0:T(1024)S(1)} %bitcast.110, f32[1024]{0:T(1024)S(1)} %bitcast.100, f32[256]{0:T(256)S(1)} %copy-done.43, ...), kind=kLoop, calls=%fused_computation.48 | loop fusion | flops 5242880 | bytes 3188736 | tf_op jit(solution)/shard_map/convert_element_type | solution.py:62
  218.3 136.4 %all-reduce.7.cloned.1.call-done = (f32[64,128]{1,0:T(8,128)}, f32[3,3,1024]{2,1,0:T(4,128)}) async-done(((f32[64,128]{1,0:T(8,128)}, f32[3,3,1024]{2,1,0:T(4,128)}), (f32[64,128]{1,0:T(8,128)}, f32[3,3,1024]{2,1,0:T(4,128)})) %all-reduce.7.cloned.1.call-update) | async-done | bytes 69648 | tf_op jit(solution)/shard_map/psum | solution.py:181
  354.7 1.4 copy.40
  356.0 1.4 copy.41
  (159 shorter events, 24.1 us)
Async XLA Ops:
  7.2 347.5 %all-reduce.7.cloned.1.call-start = ((), (), s32[]{:S(2)}) async-start(), calls=%async_computation | async-start | bytes 163840 | tf_op jit(solution)/shard_map/psum | solution.py:181
  8.2 69.4 %collective-permute-start.3 = (bf16[129,1024]{1,0:T(8,128)(2,1)S(1)}, bf16[129,1024]{1,0:T(8,128)(2,1)S(1)}, u32[]{:S(2)}, u32[]{:S(2)}) collective-permute-start(bf16[129,1024]{1,0:T(8,128)(2,1)S(1)} %slice.289), channel_id=1, source_target_pairs={{0,8},{8,16},{16,24},{24,32},{32,40},{40,48},{48,56},{56,64},{64,7... | collective-permute-start | bytes 792584 | tf_op jit(solution)/shard_map/ppermute | solution.py:14
  12.8 63.1 %collective-permute-start.5 = (s32[127]{0:T(128)S(1)}, s32[127]{0:T(128)S(1)}, u32[]{:S(2)}, u32[]{:S(2)}) collective-permute-start(s32[127]{0:T(128)S(1)} %slice.308), channel_id=1, source_target_pairs={{8,0},{16,8},{24,16},{32,24},{40,32},{48,40},{56,48},{64,56},{72,6... | collective-permute-start | bytes 1532 | tf_op jit(solution)/shard_map/ppermute | solution.py:14
  14.1 61.8 %collective-permute-start.1 = (s32[129]{0:T(256)S(1)}, s32[129]{0:T(256)S(1)}, u32[]{:S(2)}, u32[]{:S(2)}) collective-permute-start(s32[129]{0:T(256)S(1)} %slice.273), channel_id=1, source_target_pairs={{0,8},{8,16},{16,24},{24,32},{32,40},{40,48},{48,56},{56,64},{64,7... | collective-permute-start | bytes 1556 | tf_op jit(solution)/shard_map/ppermute | solution.py:14
  20.0 68.5 %collective-permute-start = (bf16[2,1024]{1,0:T(2,128)(2,1)}, bf16[2,1024]{1,0:T(2,128)(2,1)}, u32[]{:S(2)}, u32[]{:S(2)}) collective-permute-start(bf16[2,1024]{1,0:T(2,128)(2,1)} %slice.271), channel_id=1, source_target_pairs={{0,8},{8,16},{16,24},{24,32},{32,40},{40,48},{48,56},{56,64},{64,7... | collective-permute-start | bytes 12296 | tf_op jit(solution)/shard_map/ppermute | solution.py:14
  25.4 52.2 %collective-permute-start.2 = (bf16[129,1024]{1,0:T(8,128)(2,1)S(1)}, bf16[129,1024]{1,0:T(8,128)(2,1)S(1)}, u32[]{:S(2)}, u32[]{:S(2)}) collective-permute-start(bf16[129,1024]{1,0:T(8,128)(2,1)S(1)} %slice.279), channel_id=1, source_target_pairs={{0,8},{8,16},{16,24},{24,32},{32,40},{40,48},{48,56},{56,64},{64,7... | collective-permute-start | bytes 792584 | tf_op jit(solution)/shard_map/ppermute | solution.py:14
  31.4 46.2 %copy-start.23 = (f32[1,1,1024]{2,1,0:T(1,128)}, f32[1,1,1024]{2,1,0:T(1,128)S(1)}, u32[]{:S(2)}) copy-start(f32[1,1,1024]{2,1,0:T(1,128)S(1)} %get-tuple-element.40) | copy-start | bytes 12292
  31.4 46.3 %copy-start.25 = (f32[1,1,1024]{2,1,0:T(1,128)}, f32[1,1,1024]{2,1,0:T(1,128)S(1)}, u32[]{:S(2)}) copy-start(f32[1,1,1024]{2,1,0:T(1,128)S(1)} %get-tuple-element.41) | copy-start | bytes 12292
  31.4 46.3 %copy-start.27 = (f32[1,1,1024]{2,1,0:T(1,128)}, f32[1,1,1024]{2,1,0:T(1,128)S(1)}, u32[]{:S(2)}) copy-start(f32[1,1,1024]{2,1,0:T(1,128)S(1)} %get-tuple-element.42) | copy-start | bytes 12292
  31.4 46.3 %copy-start.29 = (f32[1,1,1024]{2,1,0:T(1,128)}, f32[1,1,1024]{2,1,0:T(1,128)S(1)}, u32[]{:S(2)}) copy-start(f32[1,1,1024]{2,1,0:T(1,128)S(1)} %get-tuple-element.43) | copy-start | bytes 12292
  31.4 46.3 %copy-start.31 = (f32[1,1,1024]{2,1,0:T(1,128)}, f32[1,1,1024]{2,1,0:T(1,128)S(1)}, u32[]{:S(2)}) copy-start(f32[1,1,1024]{2,1,0:T(1,128)S(1)} %get-tuple-element.46) | copy-start | bytes 12292
  31.4 46.3 %copy-start.33 = (f32[1,1,1024]{2,1,0:T(1,128)}, f32[1,1,1024]{2,1,0:T(1,128)S(1)}, u32[]{:S(2)}) copy-start(f32[1,1,1024]{2,1,0:T(1,128)S(1)} %get-tuple-element.47) | copy-start | bytes 12292
  38.1 16.1 %copy-start.45 = (bf16[1024]{0:T(1024)(128)(2,1)S(1)}, bf16[1024]{0:T(1024)(128)(2,1)}, u32[]{:S(2)}) copy-start(bf16[1024]{0:T(1024)(128)(2,1)} %param.13) | copy-start | bytes 6148
  60.0 16.0 %copy-start.44 = (s32[256]{0:T(256)S(1)}, s32[256]{0:T(256)}, u32[]{:S(2)}) copy-start(s32[256]{0:T(256)} %param.12) | copy-start | bytes 3076
  60.0 17.7 %copy-start.12 = (bf16[256,1024]{1,0:T(8,128)(2,1)S(1)}, bf16[256,1024]{1,0:T(8,128)(2,1)}, u32[]{:S(2)}) copy-start(bf16[256,1024]{1,0:T(8,128)(2,1)} %param.10) | copy-start | bytes 1572868
  60.0 17.7 %copy-start.13 = (bf16[256,1024]{1,0:T(8,128)(2,1)S(1)}, bf16[256,1024]{1,0:T(8,128)(2,1)}, u32[]{:S(2)}) copy-start(bf16[256,1024]{1,0:T(8,128)(2,1)} %param.9) | copy-start | bytes 1572868
  77.6 5.0 %copy-start.15 = (bf16[129,1024]{1,0:T(8,128)(2,1)}, bf16[129,1024]{1,0:T(8,128)(2,1)S(1)}, u32[]{:S(2)}) copy-start(bf16[129,1024]{1,0:T(8,128)(2,1)S(1)} %collective-permute-done.2) | copy-start | bytes 792580
  88.5 14.9 %copy-start.4 = (f32[128,1024]{1,0:T(8,128)}, f32[128,1024]{1,0:T(8,128)S(1)}, u32[]{:S(2)}) copy-start(f32[128,1024]{1,0:T(8,128)S(1)} %copy.26) | copy-start | bytes 1572868
  88.5 13.3 %copy-start.2 = (bf16[256,1024]{1,0:T(8,128)(2,1)S(1)}, bf16[256,1024]{1,0:T(8,128)(2,1)}, u32[]{:S(2)}) copy-start(bf16[256,1024]{1,0:T(8,128)(2,1)} %param.11) | copy-start | bytes 1572868
  101.8 14.0 %copy-start.38 = (f32[256]{0:T(256)}, f32[256]{0:T(256)S(1)}, u32[]{:S(2)}) copy-start(f32[256]{0:T(256)S(1)} %add_rsqrt_fusion) | copy-start | bytes 3076
  115.8 4.3 %copy-start.35 = (f32[1024]{0:T(1024)S(1)}, f32[1024]{0:T(1024)}, u32[]{:S(2)}) copy-start(f32[1024]{0:T(1024)} %get-tuple-element.15) | copy-start | bytes 12292
  118.8 67.7 %collective-permute-start.4 = (bf16[127,1024]{1,0:T(8,128)(2,1)}, bf16[127,1024]{1,0:T(8,128)(2,1)}, u32[]{:S(2)}, u32[]{:S(2)}) collective-permute-start(bf16[127,1024]{1,0:T(8,128)(2,1)} %slice.353), channel_id=1, source_target_pairs={{8,0},{16,8},{24,16},{32,24},{40,32},{48,40},{56,48},{64,56},{72,6... | collective-permute-start | bytes 780296 | tf_op jit(solution)/shard_map/ppermute | solution.py:14
  120.7 12.0 %collective-permute-start.7 = (f32[1024]{0:T(1024)}, f32[1024]{0:T(1024)}, u32[]{:S(2)}, u32[]{:S(2)}) collective-permute-start(f32[1024]{0:T(1024)} %broadcast_multiply_fusion.3), channel_id=1, source_target_pairs={{0,8},{8,0},{16,24},{24,16},{32,40},{40,32},{48,56},{56,48},{64,72... | collective-permute-start | bytes 12296 | tf_op jit(solution)/shard_map/ppermute | solution.py:149
  125.1 10.6 %copy-start.6 = (bf16[255,1024]{0,1:T(8,128)(2,1)S(1)}, bf16[255,1024]{0,1:T(8,128)(2,1)}, u32[]{:S(2)}) copy-start(bf16[255,1024]{0,1:T(8,128)(2,1)} %copy-done.5) | copy-start | bytes 1566724
  134.0 23.2 %collective-permute-start.8 = (f32[1024]{0:T(1024)}, f32[1024]{0:T(1024)}, u32[]{:S(2)}, u32[]{:S(2)}) collective-permute-start(f32[1024]{0:T(1024)} %fusion.68), channel_id=1, source_target_pairs={{0,16},{8,24},{16,0},{24,8},{32,48},{40,56},{48,32},{56,40},{64,80... | collective-permute-start | bytes 12296 | tf_op jit(solution)/shard_map/ppermute | solution.py:149
  157.9 19.0 %collective-permute-start.9 = (f32[1024]{0:T(1024)S(1)}, f32[1024]{0:T(1024)S(1)}, u32[]{:S(2)}, u32[]{:S(2)}) collective-permute-start(f32[1024]{0:T(1024)S(1)} %add.99), channel_id=1, source_target_pairs={{0,32},{8,40},{16,48},{24,56},{32,0},{40,8},{48,16},{56,24},{64,96... | collective-permute-start | bytes 12296 | tf_op jit(solution)/shard_map/ppermute | solution.py:149
  176.9 3.7 %collective-permute-start.10 = (f32[1024]{0:T(1024)S(1)}, f32[1024]{0:T(1024)S(1)}, u32[]{:S(2)}, u32[]{:S(2)}) collective-permute-start(f32[1024]{0:T(1024)S(1)} %add.100), channel_id=1, source_target_pairs={{0,64},{8,72},{16,80},{24,88},{32,96},{40,104},{48,112},{56,120},{... | collective-permute-start | bytes 12296 | tf_op jit(solution)/shard_map/ppermute | solution.py:149
  180.6 5.3 %collective-permute-start.11 = (f32[1024]{0:T(1024)S(1)}, f32[1024]{0:T(1024)S(1)}, u32[]{:S(2)}, u32[]{:S(2)}) collective-permute-start(f32[1024]{0:T(1024)S(1)} %add.101), channel_id=1, source_target_pairs={{0,128},{8,136},{16,144},{24,152},{32,160},{40,168},{48,176},{56,1... | collective-permute-start | bytes 12296 | tf_op jit(solution)/shard_map/ppermute | solution.py:149
  196.1 5.6 %copy-start.19 = (f32[1024]{0:T(1024)S(1)}, f32[1024]{0:T(1024)}, u32[]{:S(2)}) copy-start(f32[1024]{0:T(1024)} %convert_element_type.293) | copy-start | bytes 12292
  196.1 5.6 %copy-start.36 = (f32[256]{0:T(256)S(1)}, f32[256]{0:T(256)}, u32[]{:S(2)}) copy-start(f32[256]{0:T(256)} %get-tuple-element.60) | copy-start | bytes 3076
  196.1 5.6 %copy-start.37 = (f32[256]{0:T(256)S(1)}, f32[256]{0:T(256)}, u32[]{:S(2)}) copy-start(f32[256]{0:T(256)} %get-tuple-element.61) | copy-start | bytes 3076
  196.1 5.6 %copy-start.39 = (f32[256]{0:T(256)S(1)}, f32[256]{0:T(256)}, u32[]{:S(2)}) copy-start(f32[256]{0:T(256)} %copy-done.38) | copy-start | bytes 3076
  196.1 5.6 %copy-start.41 = (f32[256]{0:T(256)S(1)}, f32[256]{0:T(256)}, u32[]{:S(2)}) copy-start(f32[256]{0:T(256)} %copy-done.40) | copy-start | bytes 3076
  201.8 4.2 %copy-start.8 = (f32[383,1024]{1,0:T(8,128)S(1)}, f32[383,1024]{1,0:T(8,128)}, u32[]{:S(2)}) copy-start(f32[383,1024]{1,0:T(8,128)} %get-tuple-element.28) | copy-start | bytes 4706308
  201.8 4.2 %copy-start.14 = (bf16[256,1024]{1,0:T(8,128)(2,1)S(1)}, bf16[256,1024]{1,0:T(8,128)(2,1)}, u32[]{:S(2)}) copy-start(bf16[256,1024]{1,0:T(8,128)(2,1)} %param.9) | copy-start | bytes 1572868
  201.8 4.2 %copy-start.16 = (bf16[129,1024]{1,0:T(8,128)(2,1)S(1)}, bf16[129,1024]{1,0:T(8,128)(2,1)}, u32[]{:S(2)}) copy-start(bf16[129,1024]{1,0:T(8,128)(2,1)} %copy-done.15) | copy-start | bytes 792580
  206.0 7.0 %copy-start.24 = (f32[1,1,1024]{2,1,0:T(1,128)S(1)}, f32[1,1,1024]{2,1,0:T(1,128)}, u32[]{:S(2)}) copy-start(f32[1,1,1024]{2,1,0:T(1,128)} %copy-done.23) | copy-start | bytes 12292
  206.0 7.0 %copy-start.26 = (f32[1,1,1024]{2,1,0:T(1,128)S(1)}, f32[1,1,1024]{2,1,0:T(1,128)}, u32[]{:S(2)}) copy-start(f32[1,1,1024]{2,1,0:T(1,128)} %copy-done.25) | copy-start | bytes 12292
  206.0 7.0 %copy-start.28 = (f32[1,1,1024]{2,1,0:T(1,128)S(1)}, f32[1,1,1024]{2,1,0:T(1,128)}, u32[]{:S(2)}) copy-start(f32[1,1,1024]{2,1,0:T(1,128)} %copy-done.27) | copy-start | bytes 12292
  206.0 7.0 %copy-start.30 = (f32[1,1,1024]{2,1,0:T(1,128)S(1)}, f32[1,1,1024]{2,1,0:T(1,128)}, u32[]{:S(2)}) copy-start(f32[1,1,1024]{2,1,0:T(1,128)} %copy-done.29) | copy-start | bytes 12292
  206.0 7.0 %copy-start.32 = (f32[1,1,1024]{2,1,0:T(1,128)S(1)}, f32[1,1,1024]{2,1,0:T(1,128)}, u32[]{:S(2)}) copy-start(f32[1,1,1024]{2,1,0:T(1,128)} %copy-done.31) | copy-start | bytes 12292
  206.0 7.0 %copy-start.34 = (f32[1,1,1024]{2,1,0:T(1,128)S(1)}, f32[1,1,1024]{2,1,0:T(1,128)}, u32[]{:S(2)}) copy-start(f32[1,1,1024]{2,1,0:T(1,128)} %copy-done.33) | copy-start | bytes 12292
  206.0 7.0 %copy-start.42 = (f32[256]{0:T(256)S(1)}, f32[256]{0:T(256)}, u32[]{:S(2)}) copy-start(f32[256]{0:T(256)} %get-tuple-element.48) | copy-start | bytes 3076
  206.0 7.0 %copy-start.43 = (f32[256]{0:T(256)S(1)}, f32[256]{0:T(256)}, u32[]{:S(2)}) copy-start(f32[256]{0:T(256)} %get-tuple-element.49) | copy-start | bytes 3076
  207.2 5.7 %collective-permute-start.6 = (f32[3,2,1024]{2,1,0:T(2,128)S(1)}, f32[3,2,1024]{2,1,0:T(2,128)S(1)}, u32[]{:S(2)}, u32[]{:S(2)}) collective-permute-start(f32[3,2,1024]{2,1,0:T(2,128)S(1)} %pad_maximum_fusion.9), channel_id=1, source_target_pairs={{8,0},{16,8},{24,16},{32,24},{40,32},{48,40},{56,48},{64,56},{72,6... | collective-permute-start | bytes 73736 | tf_op jit(solution)/shard_map/ppermute | solution.py:14
  213.0 4.0 %copy-start.10 = (f32[256,1024]{1,0:T(8,128)S(1)}, f32[256,1024]{1,0:T(8,128)}, u32[]{:S(2)}) copy-start(f32[256,1024]{1,0:T(8,128)} %copy-done.9) | copy-start | bytes 3145732
  213.0 4.0 %copy-start.20 = (f32[1,1,1024]{2,1,0:T(1,128)S(1)}, f32[1,1,1024]{2,1,0:T(1,128)}, u32[]{:S(2)}) copy-start(f32[1,1,1024]{2,1,0:T(1,128)} %get-tuple-element.39) | copy-start | bytes 12292
  213.1 4.0 %copy-start.21 = (f32[1,1,1024]{2,1,0:T(1,128)S(1)}, f32[1,1,1024]{2,1,0:T(1,128)}, u32[]{:S(2)}) copy-start(f32[1,1,1024]{2,1,0:T(1,128)} %get-tuple-element.44) | copy-start | bytes 12292
  (11 other events, 28.9 us)
Sparse Core Ops, SparseCore 0:
  209.4 145.2 all-reduce.6
